TPU v7x, 128 devices: a whole 4x4x4 slice. The times are simulated.
128 devices in a mesh: cfg: 2 (over core), lat: 4 (over x), seq: 16 (over z, y).
Axes of the slice: x: 4, y: 4, z: 4, core: 2. Of those that a mesh axis runs over, the one named last changes fastest.
Arguments:
- latents: float32 [24, 1024, 16], P('lat', 'seq'), may hold values from -6 to 6
- timesteps: int32 [24], P('lat'), may hold values from 0 to 999
- labels: int32 [24], P('lat'), may hold values from 0 to 999
- guidance: float32 [1], replicated, may hold values from 1.5 to 4
- keep_coef: float32 [24], P('lat'), may hold values from 0.8 to 1.2
- noise_coef: float32 [24], P('lat'), may hold values from -0.6 to -0.2
- w_patch: bfloat16 [16, 1152], replicated, may hold values from -1.5 to 1.5
- label_table: bfloat16 [1001, 1152], replicated, may hold values from -6 to 6
- w_time1: bfloat16 [256, 1152], P(None, 'lat'), may hold values from -0.375 to 0.375
- w_time2: bfloat16 [1152, 1152], P(None, 'lat'), may hold values from -0.1875 to 0.1875
- ada_weight: bfloat16 [1152, 9216], P(None, 'seq'), may hold values from -0.1875 to 0.1875
- w_qkv: bfloat16 [1152, 3456], P(None, 'seq'), may hold values from -2.9168155 to 2.9168155
- w_proj: bfloat16 [1152, 1152], P(None, 'seq'), may hold values from -0.1875 to 0.1875
- w_fc1: bfloat16 [1152, 4608], P(None, 'seq'), may hold values from -0.1875 to 0.1875
- w_fc2: bfloat16 [4608, 1152], P('seq'), may hold values from -0.09375 to 0.09375
- w_out: bfloat16 [1152, 16], replicated, may hold values from -0.1875 to 0.1875
Outputs:
- next_latents: float32 [24, 1024, 16], P('lat', 'seq', 'cfg')
All inputs are finite; a program needn't handle non-finite values.
Results may differ from a plain program's by a relative error of at most 0.009.
Values may be sent and summed in bfloat16 or wider, within the bound.
A program may use at most 192 MiB of HBM per device.

v0:
```python
import math
import jax
import jax.numpy as jnp
from jax import lax
from jax.sharding import PartitionSpec as P

D = 1152
HEADS = 16
HEAD_DIM = 72
CLASSES = 1000
FREQ = 256
GRID = 32


def swapped(value, axis, stride):
    mask = 2**stride
    pairs = [(source, source ^ mask) for source in range(lax.axis_size(axis))]
    return lax.ppermute(value, axis, pairs)


def layer_norm(values):
    average = jnp.mean(values, axis=-1, keepdims=True)
    centered = values - average
    spread = jnp.mean(centered * centered, axis=-1, keepdims=True)
    return centered * lax.rsqrt(spread + 1e-06)


def modulate(values, shifted, scaled):
    return layer_norm(values) * (1.0 + scaled[:, None, :]) + shifted[:, None, :]


def time_waves(timesteps):
    half_count = FREQ // 2
    frequency = jnp.exp(-math.log(10000.0) * jnp.arange(half_count, dtype=jnp.float32) / half_count)
    angles = timesteps.astype(jnp.float32)[:, None] * frequency[None, :]
    return jnp.concatenate([jnp.cos(angles), jnp.sin(angles)], axis=-1)


def grid_waves(positions):
    quarter = D // 4
    frequency = jnp.exp(-math.log(10000.0) * jnp.arange(quarter, dtype=jnp.float32) / quarter)
    column = (positions % GRID).astype(jnp.float32)[:, None] * frequency[None, :]
    row_angle = (positions // GRID).astype(jnp.float32)[:, None] * frequency[None, :]
    return jnp.concatenate(
        [jnp.sin(column), jnp.cos(column), jnp.sin(row_angle), jnp.cos(row_angle)], axis=-1
    )


def condition(timesteps, classes, label_table, w_time1, w_time2):
    waves = time_waves(timesteps).astype(jnp.bfloat16)
    hidden_time = jax.nn.silu(jnp.dot(waves, w_time1, preferred_element_type=jnp.float32)).astype(
        jnp.bfloat16
    )
    time_vector = jnp.dot(hidden_time, w_time2, preferred_element_type=jnp.float32)
    onehot = (classes[:, None] == jnp.arange(CLASSES + 1, dtype=jnp.int32)[None, :]).astype(
        jnp.bfloat16
    )
    return time_vector + jnp.dot(onehot, label_table, preferred_element_type=jnp.float32)


def shards(
    latents,
    timesteps,
    labels,
    guidance,
    keep_coef,
    noise_coef,
    w_patch,
    label_table,
    w_time1,
    w_time2,
    ada_weight,
    w_qkv,
    w_proj,
    w_fc1,
    w_fc2,
    w_out,
):
    lat_count, tok_count, channels = latents.shape
    model_width = w_patch.shape[1]
    side_index = lax.axis_index("cfg")
    classes = jnp.where(side_index == 0, labels, CLASSES)
    time_first, time_second = (
        lax.all_gather(w_time1, "lat", axis=1, tiled=True),
        lax.all_gather(w_time2, "lat", axis=1, tiled=True),
    )
    conditioning = condition(timesteps, classes, label_table, time_first, time_second)
    own_columns = jnp.dot(
        jax.nn.silu(conditioning).astype(jnp.bfloat16),
        ada_weight,
        preferred_element_type=jnp.float32,
    )
    modulation = lax.all_gather(own_columns, "seq", axis=1, tiled=True)
    pieces = [
        modulation[:, number * model_width : (number + 1) * model_width] for number in range(8)
    ]
    positions = lax.axis_index("seq") * tok_count + jnp.arange(tok_count, dtype=jnp.int32)
    state = jnp.dot(
        latents.reshape(-1, channels).astype(jnp.bfloat16),
        w_patch,
        preferred_element_type=jnp.float32,
    )
    state = state.reshape(lat_count, tok_count, model_width) + grid_waves(positions)[None]
    qkv_full, proj_full = (
        lax.all_gather(w_qkv, "seq", axis=1, tiled=True),
        lax.all_gather(w_proj, "seq", axis=1, tiled=True),
    )
    normed = modulate(state, pieces[0], pieces[1]).astype(jnp.bfloat16).reshape(-1, model_width)
    triple = jnp.dot(normed, qkv_full, preferred_element_type=jnp.float32).astype(jnp.bfloat16)
    queries = triple[:, :model_width].reshape(lat_count, tok_count, HEADS, HEAD_DIM)
    keys_own = triple[:, model_width : 2 * model_width].reshape(lat_count, tok_count, model_width)
    values_own = triple[:, 2 * model_width :].reshape(lat_count, tok_count, model_width)
    factor = 1.0 / math.sqrt(HEAD_DIM)
    row_best = jnp.full((lat_count, HEADS, tok_count), -1e30, jnp.float32)
    keys_part = lax.all_gather(keys_own, "seq", axis=1, tiled=True)
    values_part = lax.all_gather(values_own, "seq", axis=1, tiled=True)
    key_count = keys_part.shape[1]
    keys_heads = keys_part.reshape(lat_count, key_count, HEADS, HEAD_DIM)
    values_heads = values_part.reshape(lat_count, key_count, HEADS, HEAD_DIM)
    scores = (
        jnp.einsum("lqhd,lkhd->lhqk", queries, keys_heads, preferred_element_type=jnp.float32)
        * factor
    )
    raised = jnp.maximum(row_best, jnp.max(scores, axis=-1))
    exponent = jnp.exp(scores - raised[..., None])
    row_sums = jnp.sum(exponent, axis=-1)
    weighted = jnp.einsum(
        "lhqk,lkhd->lhqd",
        exponent.astype(jnp.bfloat16),
        values_heads,
        preferred_element_type=jnp.float32,
    )
    row_best, row_sums, weighted = (raised, row_sums, weighted)
    attended = (
        (weighted / row_sums[..., None])
        .transpose(0, 2, 1, 3)
        .reshape(-1, model_width)
        .astype(jnp.bfloat16)
    )
    projected = jnp.dot(attended, proj_full, preferred_element_type=jnp.float32)
    state = state + pieces[2][:, None, :] * projected.reshape(lat_count, tok_count, model_width)
    normed = modulate(state, pieces[3], pieces[4]).astype(jnp.bfloat16).reshape(-1, model_width)
    fc1_full, fc2_full = (
        lax.all_gather(w_fc1, "seq", axis=1, tiled=True),
        lax.all_gather(w_fc2, "seq", axis=0, tiled=True),
    )
    hidden = jax.nn.gelu(
        jnp.dot(normed, fc1_full, preferred_element_type=jnp.float32), approximate=True
    ).astype(jnp.bfloat16)
    mlp_out = jnp.dot(hidden, fc2_full, preferred_element_type=jnp.float32)
    state = state + pieces[5][:, None, :] * mlp_out.reshape(lat_count, tok_count, model_width)
    final = modulate(state, pieces[6], pieces[7]).astype(jnp.bfloat16).reshape(-1, model_width)
    noise_own = jnp.dot(final, w_out, preferred_element_type=jnp.float32).reshape(
        lat_count, tok_count, channels
    )
    half_width = channels // 2
    own_latent = lax.dynamic_slice_in_dim(latents, side_index * half_width, half_width, 2)
    partner = swapped(noise_own, "cfg", 0)
    cond_noise = jnp.where(side_index == 0, noise_own, partner)
    free_noise = jnp.where(side_index == 0, partner, noise_own)
    combined = free_noise + guidance[0] * (cond_noise - free_noise)
    guided = lax.dynamic_slice_in_dim(combined, side_index * half_width, half_width, 2)
    return keep_coef[:, None, None] * own_latent + noise_coef[:, None, None] * guided


def solution(mesh):
    return jax.shard_map(
        shards,
        mesh=mesh,
        in_specs=(
            P("lat", "seq", None),
            P("lat"),
            P("lat"),
            P(),
            P("lat"),
            P("lat"),
            P(),
            P(),
            P(None, "lat"),
            P(None, "lat"),
            P(None, "seq"),
            P(None, "seq"),
            P(None, "seq"),
            P(None, "seq"),
            P("seq", None),
            P(),
        ),
        out_specs=P("lat", "seq", "cfg"),
        check_vma=False,
    )
```

profile of v0, /device:TPU:1, one launch (start us, length us, event | category | flops | bytes accessed | tf_op | source)
XLA Modules:
  0.0 571.2 jit_solution(164010904563712114)
XLA Ops:
  6.5 0.7 all-gather.9.cloned.1.call-update
  7.3 0.7 all-gather.11.cloned.1.call-update
  8.1 0.7 convert_element_type.57
  8.7 0.8 multiply_cosine_fusion
  9.5 0.2 concatenate.7
  9.7 1.3 fusion.61
  11.0 1.2 copy-done.2
  12.2 0.3 multiply_reduce_fusion.3
  12.6 12.5 %all_gather.27 = bf16[256,1152]{0,1:T(8,128)(2,1)S(1)} all-gather(bf16[256,288]{0,1:T(8,128)(2,1)S(1)} %copy-done.5), channel_id=1, replica_groups=mesh['cfg'=2,'lat'=4,'seq'=16] {'lat'}, dimensions={1}, use_global_device_ids=true | all-gather | bytes 737280 | tf_op jit(solution)/shard_map/all_gather | solution.py:84
  25.1 0.1 fusion.36
  25.2 23.4 %all-gather.9.cloned.1.call-done = bf16[1152,1152]{0,1:T(8,128)(2,1)} async-done(((bf16[1152,288]{0,1:T(8,128)(2,1)}), bf16[1152,1152]{0,1:T(8,128)(2,1)}) %all-gather.9.cloned.1.call-update) | async-done | bytes 2654224 | tf_op jit(solution)/shard_map/all_gather | solution.py:85
  48.6 2.7 fusion.31
  51.3 2.1 convolution_bitcast_fusion
  53.5 21.0 %all-gather = f32[16,576,6]{1,2,0:T(8,128)S(1)} all-gather(f32[1,576,6]{1,2,0:T(8,128)S(1)} %convolution_bitcast_fusion), channel_id=1, replica_groups=mesh['cfg'=2,'lat'=4,'seq'=16] {'seq'}, dimensions={0}, use_global_device_ids=true | all-gather | bytes 235008 | tf_op jit(solution)/shard_map/all_gather | solution.py:93
  74.5 0.1 reshape.145
  74.7 0.5 add_convert_fusion.2
  75.1 45.3 %all-gather.11.cloned.1.call-done = bf16[1152,3456]{0,1:T(8,128)(2,1)} async-done(((bf16[1152,216]{0,1:T(8,128)(2,1)}), bf16[1152,3456]{0,1:T(8,128)(2,1)}) %all-gather.11.cloned.1.call-update) | async-done | bytes 7962640 | tf_op jit(solution)/shard_map/all_gather | solution.py:105
  120.4 8.3 %convolution_convert_fusion = bf16[384,3456]{1,0:T(8,128)(2,1)S(1)} fusion(bf16[384,1152]{1,0:T(8,128)(2,1)S(1)} %bitcast.55, bf16[1152,3456]{0,1:T(8,128)(2,1)} %all-gather.11.cloned.1.call-done), kind=kOutput, calls=%fused_computation.16 | convolution fusion | flops 3058974720 | bytes 11501568 | tf_op jit(solution)/shard_map/dot_general | solution.py:109
  128.7 1.5 fusion.60
  130.2 0.0 all-gather.15.cloned.1.call-start
  130.2 0.5 all-gather.15.cloned.1.call-update
  130.8 0.5 all-gather.17.cloned.1.call-update
  131.4 0.5 all-gather.19.cloned.1.call-update
  131.9 0.2 all-gather.21.cloned.1.call-start
  132.1 0.5 all-gather.21.cloned.1.call-update
  132.6 3.6 reshape.137
  136.3 91.6 %all-gather.13.cloned.1.call-done = bf16[6,1024,1152]{2,1,0:T(8,128)(2,1)} async-done(((bf16[6,64,1152]{2,1,0:T(8,128)(2,1)}), bf16[6,1024,1152]{2,1,0:T(8,128)(2,1)}) %all-gather.13.cloned.1.call-update) | async-done | bytes 14155792 | tf_op jit(solution)/shard_map/all_gather | solution.py:115
  227.9 18.7 %copy.27 = bf16[6,1024,1152]{1,2,0:T(8,128)(2,1)} copy(bf16[6,1024,1152]{2,1,0:T(8,128)(2,1)} %all-gather.13.cloned.1.call-done) | data formatting | bytes 28311552 | tf_op jit(solution)/shard_map/all_gather | solution.py:115
  246.7 80.9 %all-gather.15.cloned.1.call-done = bf16[6,1024,1152]{2,1,0:T(8,128)(2,1)} async-done(((bf16[6,64,1152]{2,1,0:T(8,128)(2,1)}), bf16[6,1024,1152]{2,1,0:T(8,128)(2,1)}) %all-gather.15.cloned.1.call-update) | async-done | bytes 14155792 | tf_op jit(solution)/shard_map/all_gather | solution.py:116
  327.6 18.7 %copy.29 = bf16[6,1024,1152]{1,2,0:T(8,128)(2,1)} copy(bf16[6,1024,1152]{2,1,0:T(8,128)(2,1)} %all-gather.15.cloned.1.call-done) | data formatting | bytes 28311552 | tf_op jit(solution)/shard_map/all_gather | solution.py:116
  346.3 18.5 %multiply_reduce_fusion = (f32[6,16,64]{2,1,0:T(8,128)S(1)}, f32[6,16,64,1024]{3,2,1,0:T(8,128)}) fusion(bf16[6,1024,16,72]{1,3,2,0:T(8,128)(2,1)} %bitcast.48, bf16[6,64,16,72]{3,2,1,0:T(8,128)(2,1)} %reshape.137), kind=kOutput, calls=%fused_computation.1 | convolution fusion | flops 918546432 | bytes 40230912 | tf_op jit(solution)/shard_map/lqhd,lkhd->lhqk/dot_general | solution.py:121
  364.8 11.2 %fusion = f32[6,16,64]{2,1,0:T(8,128)S(1)} fusion(f32[6,16,64,1024]{3,2,1,0:T(8,128)} %get-tuple-element.29, f32[6,16,64]{2,1,0:T(8,128)S(1)} %broadcast_maximum_fusion), kind=kLoop, calls=%fused_computation.2 | loop fusion | flops 18868224 | bytes 25214976 | tf_op jit(solution)/shard_map/reduce_sum | solution.py:126
  376.0 14.7 %fusion.20 = bf16[6,64,16,72]{3,1,2,0:T(8,128)(2,1)S(1)} fusion(bf16[6,1024,16,72]{1,3,2,0:T(8,128)(2,1)} %bitcast.49, f32[6,16,64,1024]{3,2,1,0:T(8,128)} %get-tuple-element.29, f32[6,16,64]{2,1,0:T(8,128)S(1)} %broadcast_maximum_fusion, f32[6,64,16]{1,2,0:T(8,128)S(1)} %bitcast.56), kind=kOutput, calls=%fused_computation.25 | convolution fusion | flops 925728768 | bytes 40255488 | tf_op jit(solution)/shard_map/lhqk,lkhd->lhqd/dot_general | solution.py:127
  390.8 2.2 copy.30
  393.0 3.2 convert_element_type.64
  396.2 3.3 fusion.62
  399.6 0.3 multiply_reduce_fusion.2
  400.0 0.9 copy-done.4
  400.9 0.4 add_convert_fusion.1
  401.3 56.8 %all-gather.19.cloned.1.call-done = bf16[1152,4608]{0,1:T(8,128)(2,1)} async-done(((bf16[1152,288]{0,1:T(8,128)(2,1)}), bf16[1152,4608]{0,1:T(8,128)(2,1)}) %all-gather.19.cloned.1.call-update) | async-done | bytes 10616848 | tf_op jit(solution)/shard_map/all_gather | solution.py:144
  458.1 82.9 %all-gather.21.cloned.1.call-done = bf16[4608,1152]{1,0:T(8,128)(2,1)} async-done(((bf16[288,1152]{1,0:T(8,128)(2,1)}), bf16[4608,1152]{1,0:T(8,128)(2,1)}) %all-gather.21.cloned.1.call-update) | async-done | bytes 10616848 | tf_op jit(solution)/shard_map/all_gather | solution.py:145
  540.9 17.6 %fusion.14 = f32[384,1152]{1,0:T(8,128)} fusion(bf16[4608,1152]{1,0:T(8,128)(2,1)} %all-gather.21.cloned.1.call-done, bf16[384,1152]{1,0:T(8,128)(2,1)S(1)} %bitcast.54, bf16[1152,4608]{0,1:T(8,128)(2,1)} %all-gather.19.cloned.1.call-done), kind=kOutput, calls=%fused_computation.17 | convolution fusion | flops 8169652224 | bytes 23887872 | tf_op jit(solution)/shard_map/dot_general | solution.py:150
  558.6 2.5 fusion.59
  561.1 0.3 multiply_reduce_fusion.1
  561.4 0.6 fusion.27
  562.0 0.7 collective-permute-start
  563.4 0.2 collective-permute-done
  563.6 0.7 multiply_add_fusion.1
  (40 shorter events, 0.4 us)
Async XLA Ops:
  6.5 44.8 %copy-start = (bf16[1001,1152]{1,0:T(8,128)(2,1)S(1)}, bf16[1001,1152]{1,0:T(8,128)(2,1)}, u32[]{:S(2)}) copy-start(bf16[1001,1152]{1,0:T(8,128)(2,1)} %param.23) | copy-start | bytes 6918916
  6.5 3.2 copy-start.6
  6.5 42.0 %all-gather.9.cloned.1.call-start = ((), (), s32[]{:S(2)}) async-start(), calls=%async_computation | async-start | bytes 3317760 | tf_op jit(solution)/shard_map/all_gather | solution.py:85
  7.3 113.1 %all-gather.11.cloned.1.call-start = ((), (), s32[]{:S(2)}) async-start(), calls=%async_computation.1 | async-start | bytes 8460288 | tf_op jit(solution)/shard_map/all_gather | solution.py:105
  8.0 219.9 %all-gather.13.cloned.1.call-start = ((), (), s32[]{:S(2)}) async-start(), calls=%async_computation.2 | async-start | bytes 15040512 | tf_op jit(solution)/shard_map/all_gather | solution.py:115
  9.5 3.0 copy-start.5
  9.7 15.3 %copy-start.10 = (s32[6]{0:T(128)S(1)}, s32[6]{0:T(128)}, u32[]{:S(2)}) copy-start(s32[6]{0:T(128)} %param.18) | copy-start | bytes 76
  11.0 1.2 copy-start.2
  53.5 21.2 %copy-start.3 = (f32[6,64,1152]{2,1,0:T(8,128)S(1)}, f32[6,64,1152]{2,1,0:T(8,128)}, u32[]{:S(2)}) copy-start(f32[6,64,1152]{2,1,0:T(8,128)} %copy-done.2) | copy-start | bytes 5308420
  130.2 197.4 %all-gather.15.cloned.1.call-start = ((), (), s32[]{:S(2)}) async-start(), calls=%async_computation.3 | async-start | bytes 15040512 | tf_op jit(solution)/shard_map/all_gather | solution.py:116
  130.7 265.5 %all-gather.17.cloned.1.call-start = ((), (), s32[]{:S(2)}) async-start(), calls=%async_computation.4 | async-start | bytes 2820096 | tf_op jit(solution)/shard_map/all_gather | solution.py:106
  131.3 326.7 %all-gather.19.cloned.1.call-start = ((), (), s32[]{:S(2)}) async-start(), calls=%async_computation.5 | async-start | bytes 11280384 | tf_op jit(solution)/shard_map/all_gather | solution.py:144
  131.9 409.0 %all-gather.21.cloned.1.call-start = ((), (), s32[]{:S(2)}) async-start(), calls=%async_computation.6 | async-start | bytes 11280384 | tf_op jit(solution)/shard_map/all_gather | solution.py:145
  399.6 1.3 copy-start.4
  558.6 2.9 copy-start.9
  558.6 5.7 %copy-start.1 = (bf16[1001,1152]{1,0:T(8,128)(2,1)S(1)}, bf16[1001,1152]{1,0:T(8,128)(2,1)}, u32[]{:S(2)}) copy-start(bf16[1001,1152]{1,0:T(8,128)(2,1)} %param.23) | copy-start | bytes 6918916
  561.1 2.5 copy-start.7
  561.1 2.5 copy-start.8
  562.0 1.6 collective-permute-start
Sparse Core Ops, SparseCore 0:
  9.0 39.5 all-gather.8
  50.7 69.6 all-gather.10
  130.3 97.5 all-gather.12
  229.9 97.6 all-gather.14
  329.6 45.8 all-gather.16
  377.4 80.5 all-gather.18
  460.2 80.6 all-gather.20
where the time goes:
time: 573 us; the launch traced here: 571 us
  waiting for transfers between devices  385 us (67%)
  matrix products  69.3 us (12%)
  local copies, waits for them, and re-layouts  50.5 us (9%)
  blocking collectives  33.4 us (6%)
  other arithmetic  17.8 us (3%)
  between operations  14.4 us (3%)
    all_gather x1, waiting for transfers between devices, shards(): keys_part = lax.all_gather(keys_own, 'seq', axis=1, tiled=True)  91.6 us
    all_gather x1, waiting for transfers between devices, shards(): lax.all_gather(w_fc2, 'seq', axis=0, tiled=True)  82.9 us
    all_gather x1, waiting for transfers between devices, shards(): values_part = lax.all_gather(values_own, 'seq', axis=1, tiled=True)  80.9 us
    all_gather x1, waiting for transfers between devices, shards(): lax.all_gather(w_fc1, 'seq', axis=1, tiled=True)  56.8 us
    all_gather x1, waiting for transfers between devices, shards(): lax.all_gather(w_qkv, 'seq', axis=1, tiled=True)  45.3 us
    all_gather x1, waiting for transfers between devices, shards(): lax.all_gather(w_time2, 'lat', axis=1, tiled=True)  23.4 us
    all_gather x1, blocking collectives, shards(): modulation = lax.all_gather(own_columns, 'seq', axis=1, tiled=True)  21 us
    all_gather x1, local copies, waits for them, and re-layouts, shards(): keys_part = lax.all_gather(keys_own, 'seq', axis=1, tiled=True)  18.7 us
  transfers between devices with their start and end apart: 8, of which 7 were waited for; matrix products, arithmetic and copies ran while one was open for 18% of the time, Pallas kernels for 0%

commit v1 on v0

--- a/solution.py
+++ b/solution.py
@@ -10,6 +10,11 @@
 CLASSES = 1000
 FREQ = 256
 GRID = 32
+
+
+def swapped_in(x, name, dim):
+    sent = jnp.stack([x] * lax.axis_size(name))
+    return jnp.concatenate(lax.all_to_all(sent, name, 0, 0), axis=dim)
 
 
 def swapped(value, axis, stride):
@@ -82,7 +87,7 @@
     classes = jnp.where(side_index == 0, labels, CLASSES)
     time_first, time_second = (
         lax.all_gather(w_time1, "lat", axis=1, tiled=True),
-        lax.all_gather(w_time2, "lat", axis=1, tiled=True),
+        swapped_in(w_time2, "lat", 1),
     )
     conditioning = condition(timesteps, classes, label_table, time_first, time_second)
     own_columns = jnp.dot(

time: 573 us -> 539 us (0.941)
  waiting for transfers between devices: 385 us -> 320 us
  blocking collectives: 33.4 us -> 58.5 us
    all_gather x1, waiting for transfers between devices: 45.3 us -> 0.65 us  [shards(): lax.all_gather(w_qkv, 'seq', axis=1, tiled=True)]
    all_gather x1 -> x0, waiting for transfers between devices: 23.4 us -> none  [shards(): lax.all_gather(w_time2, 'lat', axis=1, tiled=True)]
    all_gather x1, blocking collectives: 12.5 us -> 34.9 us  [shards(): lax.all_gather(w_time1, 'lat', axis=1, tiled=True)]
  transfers between devices with their start and end apart: 8 -> 8, of which waited for: 7 -> 6; matrix products, arithmetic and copies ran while one was open for 18% -> 20% of each run, Pallas kernels for 0% -> 0%
where the time goes in v1:
time: 539 us; the launch traced here: 538 us
  waiting for transfers between devices  320 us (59%)
  matrix products  68.6 us (13%)
  blocking collectives  58.5 us (11%)
  local copies, waits for them, and re-layouts  53.3 us (10%)
  other arithmetic  17.2 us (3%)
  between operations  14.4 us (3%)
  starting transfers between devices  6.02 us (1%)
    all_gather x1, waiting for transfers between devices, shards(): keys_part = lax.all_gather(keys_own, 'seq', axis=1, tiled=True)  95.5 us
    all_gather x1, waiting for transfers between devices, shards(): lax.all_gather(w_fc2, 'seq', axis=0, tiled=True)  82.7 us
    all_gather x1, waiting for transfers between devices, shards(): values_part = lax.all_gather(values_own, 'seq', axis=1, tiled=True)  81.1 us
    all_gather x1, waiting for transfers between devices, shards(): lax.all_gather(w_fc1, 'seq', axis=1, tiled=True)  56.8 us
    all_gather x1, blocking collectives, shards(): lax.all_gather(w_time1, 'lat', axis=1, tiled=True)  34.9 us
    all_gather x1, blocking collectives, shards(): modulation = lax.all_gather(own_columns, 'seq', axis=1, tiled=True)  23.6 us
    all_gather x1, local copies, waits for them, and re-layouts, shards(): keys_part = lax.all_gather(keys_own, 'seq', axis=1, tiled=True)  18.7 us
    all_gather x1, local copies, waits for them, and re-layouts, shards(): values_part = lax.all_gather(values_own, 'seq', axis=1, tiled=True)  18.7 us
  transfers between devices with their start and end apart: 8, of which 6 were waited for; matrix products, arithmetic and copies ran while one was open for 20% of the time, Pallas kernels for 0%

profile of v1, /device:TPU:1, one launch (start us, length us, event | category | flops | bytes accessed | tf_op | source)
XLA Modules:
  0.0 537.9 jit_solution(7978137057800121709)
XLA Ops:
  6.5 0.7 all-gather.8.cloned.1.call-update
  7.3 2.9 stack.2
  10.1 5.0 all-to-all-start
  15.2 0.8 multiply_cosine_fusion
  15.9 0.2 concatenate.7
  16.2 0.5 fusion.61
  16.7 1.2 copy-done.2
  17.9 0.3 multiply_reduce_fusion.3
  18.2 34.9 %all_gather.24 = bf16[256,1152]{0,1:T(8,128)(2,1)S(1)} all-gather(bf16[256,288]{0,1:T(8,128)(2,1)S(1)} %copy-done.5), channel_id=1, replica_groups=mesh['cfg'=2,'lat'=4,'seq'=16] {'lat'}, dimensions={1}, use_global_device_ids=true | all-gather | bytes 737280 | tf_op jit(solution)/shard_map/all_gather | solution.py:89
  53.1 0.1 fusion.36
  53.2 2.8 fusion.31
  56.0 2.2 convolution_bitcast_fusion
  58.2 23.6 %all-gather = f32[16,576,6]{1,2,0:T(8,128)S(1)} all-gather(f32[1,576,6]{1,2,0:T(8,128)S(1)} %convolution_bitcast_fusion), channel_id=1, replica_groups=mesh['cfg'=2,'lat'=4,'seq'=16] {'seq'}, dimensions={0}, use_global_device_ids=true | all-gather | bytes 235008 | tf_op jit(solution)/shard_map/all_gather | solution.py:98
  81.9 0.1 reshape.155
  82.0 0.5 add_convert_fusion.2
  82.5 0.6 all-gather.8.cloned.1.call-done
  83.1 8.3 %convolution_convert_fusion = bf16[384,3456]{1,0:T(8,128)(2,1)S(1)} fusion(bf16[384,1152]{1,0:T(8,128)(2,1)S(1)} %bitcast.58, bf16[1152,3456]{0,1:T(8,128)(2,1)} %all-gather.8.cloned.1.call-done), kind=kOutput, calls=%fused_computation.16 | convolution fusion | flops 3058974720 | bytes 11501568 | tf_op jit(solution)/shard_map/dot_general | solution.py:114
  91.4 1.5 fusion.60
  92.9 0.0 all-gather.12.cloned.1.call-start
  93.0 0.7 all-gather.12.cloned.1.call-update
  93.6 0.0 all-gather.14.cloned.1.call-start
  93.7 0.5 all-gather.14.cloned.1.call-update
  94.3 0.5 all-gather.16.cloned.1.call-update
  94.8 0.2 all-gather.18.cloned.1.call-start
  95.0 0.3 all-gather.18.cloned.1.call-update
  95.4 3.7 reshape.147
  99.0 95.5 %all-gather.10.cloned.1.call-done = bf16[6,1024,1152]{2,1,0:T(8,128)(2,1)} async-done(((bf16[6,64,1152]{2,1,0:T(8,128)(2,1)}), bf16[6,1024,1152]{2,1,0:T(8,128)(2,1)}) %all-gather.10.cloned.1.call-update) | async-done | bytes 14155792 | tf_op jit(solution)/shard_map/all_gather | solution.py:120
  194.6 18.7 %copy.28 = bf16[6,1024,1152]{1,2,0:T(8,128)(2,1)} copy(bf16[6,1024,1152]{2,1,0:T(8,128)(2,1)} %all-gather.10.cloned.1.call-done) | data formatting | bytes 28311552 | tf_op jit(solution)/shard_map/all_gather | solution.py:120
  213.3 81.1 %all-gather.12.cloned.1.call-done = bf16[6,1024,1152]{2,1,0:T(8,128)(2,1)} async-done(((bf16[6,64,1152]{2,1,0:T(8,128)(2,1)}), bf16[6,1024,1152]{2,1,0:T(8,128)(2,1)}) %all-gather.12.cloned.1.call-update) | async-done | bytes 14155792 | tf_op jit(solution)/shard_map/all_gather | solution.py:121
  294.4 18.7 %copy.30 = bf16[6,1024,1152]{1,2,0:T(8,128)(2,1)} copy(bf16[6,1024,1152]{2,1,0:T(8,128)(2,1)} %all-gather.12.cloned.1.call-done) | data formatting | bytes 28311552 | tf_op jit(solution)/shard_map/all_gather | solution.py:121
  313.1 18.5 %multiply_reduce_fusion = (f32[6,16,64]{2,1,0:T(8,128)S(1)}, f32[6,16,64,1024]{3,2,1,0:T(8,128)}) fusion(bf16[6,1024,16,72]{1,3,2,0:T(8,128)(2,1)} %bitcast.51, bf16[6,64,16,72]{3,2,1,0:T(8,128)(2,1)} %reshape.147), kind=kOutput, calls=%fused_computation.1 | convolution fusion | flops 918546432 | bytes 40230912 | tf_op jit(solution)/shard_map/lqhd,lkhd->lhqk/dot_general | solution.py:126
  331.6 11.2 %fusion = f32[6,16,64]{2,1,0:T(8,128)S(1)} fusion(f32[6,16,64,1024]{3,2,1,0:T(8,128)} %get-tuple-element.29, f32[6,16,64]{2,1,0:T(8,128)S(1)} %broadcast_maximum_fusion), kind=kLoop, calls=%fused_computation.2 | loop fusion | flops 18868224 | bytes 25214976 | tf_op jit(solution)/shard_map/reduce_sum | solution.py:131
  342.8 14.8 %fusion.20 = bf16[6,64,16,72]{3,1,2,0:T(8,128)(2,1)S(1)} fusion(bf16[6,1024,16,72]{1,3,2,0:T(8,128)(2,1)} %bitcast.52, f32[6,16,64,1024]{3,2,1,0:T(8,128)} %get-tuple-element.29, f32[6,16,64]{2,1,0:T(8,128)S(1)} %broadcast_maximum_fusion, f32[6,64,16]{1,2,0:T(8,128)S(1)} %bitcast.59), kind=kOutput, calls=%fused_computation.25 | convolution fusion | flops 925728768 | bytes 40255488 | tf_op jit(solution)/shard_map/lhqk,lkhd->lhqd/dot_general | solution.py:132
  357.6 2.2 copy.31
  359.8 3.2 convert_element_type.64
  363.1 3.3 fusion.62
  366.5 0.3 multiply_reduce_fusion.2
  366.8 0.9 copy-done.4
  367.7 0.4 add_convert_fusion.1
  368.1 56.8 %all-gather.16.cloned.1.call-done = bf16[1152,4608]{0,1:T(8,128)(2,1)} async-done(((bf16[1152,288]{0,1:T(8,128)(2,1)}), bf16[1152,4608]{0,1:T(8,128)(2,1)}) %all-gather.16.cloned.1.call-update) | async-done | bytes 10616848 | tf_op jit(solution)/shard_map/all_gather | solution.py:149
  424.9 82.7 %all-gather.18.cloned.1.call-done = bf16[4608,1152]{1,0:T(8,128)(2,1)} async-done(((bf16[288,1152]{1,0:T(8,128)(2,1)}), bf16[4608,1152]{1,0:T(8,128)(2,1)}) %all-gather.18.cloned.1.call-update) | async-done | bytes 10616848 | tf_op jit(solution)/shard_map/all_gather | solution.py:150
  507.6 17.6 %fusion.14 = f32[384,1152]{1,0:T(8,128)} fusion(bf16[4608,1152]{1,0:T(8,128)(2,1)} %all-gather.18.cloned.1.call-done, bf16[384,1152]{1,0:T(8,128)(2,1)S(1)} %bitcast.57, bf16[1152,4608]{0,1:T(8,128)(2,1)} %all-gather.16.cloned.1.call-done), kind=kOutput, calls=%fused_computation.17 | convolution fusion | flops 8169652224 | bytes 23887872 | tf_op jit(solution)/shard_map/dot_general | solution.py:155
  525.3 2.5 fusion.59
  527.8 0.3 multiply_reduce_fusion.1
  528.1 0.6 fusion.27
  528.7 0.7 collective-permute-start
  530.1 0.2 collective-permute-done
  530.3 0.7 multiply_add_fusion.1
  (44 shorter events, 0.3 us)
Async XLA Ops:
  6.5 49.5 %copy-start = (bf16[1001,1152]{1,0:T(8,128)(2,1)S(1)}, bf16[1001,1152]{1,0:T(8,128)(2,1)}, u32[]{:S(2)}) copy-start(bf16[1001,1152]{1,0:T(8,128)(2,1)} %param.23) | copy-start | bytes 6918916
  6.5 76.6 %all-gather.8.cloned.1.call-start = ((), (), s32[]{:S(2)}) async-start(), calls=%async_computation.1 | async-start | bytes 8460288 | tf_op jit(solution)/shard_map/all_gather | solution.py:110
  10.1 5.0 copy-start.11
  10.1 6.0 %copy-start.6 = (f32[6,64,16]{1,2,0:T(8,128)S(1)}, f32[6,64,16]{1,2,0:T(8,128)}, u32[]{:S(2)}) copy-start(f32[6,64,16]{1,2,0:T(8,128)} %param.16) | copy-start | bytes 73732
  10.1 6.0 %copy-start.7 = (bf16[16,1152]{1,0:T(8,128)(2,1)S(1)}, bf16[16,1152]{1,0:T(8,128)(2,1)}, u32[]{:S(2)}) copy-start(bf16[16,1152]{1,0:T(8,128)(2,1)} %param.22) | copy-start | bytes 110596
  10.1 43.1 %all-to-all-start = ((bf16[4,1152,288]{1,2,0:T(8,128)(2,1)}), bf16[4,1152,288]{1,2,0:T(8,128)(2,1)}, u32[]{:S(2)}, u32[]{:S(2)}) async-start(bf16[4,1152,288]{1,2,0:T(8,128)(2,1)} %stack.2), calls=%async_computation | async-start | bytes 5308416 | tf_op jit(solution)/shard_map/all_to_all | solution.py:17
  15.1 179.5 %all-gather.10.cloned.1.call-start = ((), (), s32[]{:S(2)}) async-start(), calls=%async_computation.2 | async-start | bytes 15040512 | tf_op jit(solution)/shard_map/all_gather | solution.py:120
  15.9 2.3 copy-start.5
  16.1 36.9 %copy-start.12 = (s32[6]{0:T(128)S(1)}, s32[6]{0:T(128)}, u32[]{:S(2)}) copy-start(s32[6]{0:T(128)} %param.18) | copy-start | bytes 76
  16.7 1.2 copy-start.2
  58.2 23.8 %copy-start.3 = (f32[6,64,1152]{2,1,0:T(8,128)S(1)}, f32[6,64,1152]{2,1,0:T(8,128)}, u32[]{:S(2)}) copy-start(f32[6,64,1152]{2,1,0:T(8,128)} %copy-done.2) | copy-start | bytes 5308420
  92.9 201.5 %all-gather.12.cloned.1.call-start = ((), (), s32[]{:S(2)}) async-start(), calls=%async_computation.3 | async-start | bytes 15040512 | tf_op jit(solution)/shard_map/all_gather | solution.py:121
  93.6 269.4 %all-gather.14.cloned.1.call-start = ((), (), s32[]{:S(2)}) async-start(), calls=%async_computation.4 | async-start | bytes 2820096 | tf_op jit(solution)/shard_map/all_gather | solution.py:111
  94.2 330.7 %all-gather.16.cloned.1.call-start = ((), (), s32[]{:S(2)}) async-start(), calls=%async_computation.5 | async-start | bytes 11280384 | tf_op jit(solution)/shard_map/all_gather | solution.py:149
  94.8 412.8 %all-gather.18.cloned.1.call-start = ((), (), s32[]{:S(2)}) async-start(), calls=%async_computation.6 | async-start | bytes 11280384 | tf_op jit(solution)/shard_map/all_gather | solution.py:150
  366.4 1.3 copy-start.4
  525.3 2.9 copy-start.10
  525.3 5.7 %copy-start.1 = (bf16[1001,1152]{1,0:T(8,128)(2,1)S(1)}, bf16[1001,1152]{1,0:T(8,128)(2,1)}, u32[]{:S(2)}) copy-start(bf16[1001,1152]{1,0:T(8,128)(2,1)} %param.23) | copy-start | bytes 6918916
  527.8 2.5 copy-start.8
  527.8 2.5 copy-start.9
  528.7 1.6 collective-permute-start
Sparse Core Ops, SparseCore 0:
  9.5 73.5 all-gather.7
  93.0 101.5 all-gather.9
  196.7 97.6 all-gather.11
  296.4 45.8 all-gather.13
  344.3 80.5 all-gather.15
  426.9 80.6 all-gather.17
